TPU v7x, 32 devices: a whole 2x2x4 slice. The times are simulated.
32 devices in a mesh: chan: 8 (over y, x, core), seq: 4 (over z).
Axes of the slice: x: 2, y: 2, z: 4, core: 2. Of those that a mesh axis runs over, the one named last changes fastest.
Arguments:
- value: bfloat16 [8, 128, 32768], P('seq', 'chan'), may hold values from -6 to 6
- gate_in: bfloat16 [8, 128, 32768], P('seq', 'chan'), may hold values from -6 to 6
- gate_out: bfloat16 [8, 128, 32768], P('seq', 'chan'), may hold values from -6 to 6
- cotangent: bfloat16 [8, 128, 32768], P('seq', 'chan'), may hold values from -6 to 6
- skip_gain: float32 [128], P('chan'), may hold values from 0.25 to 1.5
- weight_in: float32 [64, 33], replicated, may hold values from -1 to 1
- bias_in: float32 [64], replicated, may hold values from -1 to 1
- weight_mid: float32 [2, 64, 64], replicated, may hold values from -0.75 to 0.75
- bias_mid: float32 [2, 64], replicated, may hold values from -1 to 1
- weight_out: float32 [128, 64], replicated, may hold values from -0.75 to 0.75
- decay_rate: float32 [128], replicated, may hold values from 3 to 15
Outputs:
- grad_value: bfloat16 [8, 128, 32768], P('seq', 'chan')
- grad_gate_in: bfloat16 [8, 128, 32768], P('seq', 'chan')
- grad_gate_out: bfloat16 [8, 128, 32768], P('seq', 'chan')
- grad_skip: float32 [128], P('chan')
- grad_weight_in: float32 [64, 33], replicated
- grad_bias_in: float32 [64], replicated
- grad_weight_mid: float32 [2, 64, 64], replicated
- grad_bias_mid: float32 [2, 64], replicated
- grad_weight_out: float32 [128, 64], replicated
- grad_rate: float32 [128], replicated
All inputs are finite; a program needn't handle non-finite values.
Results may differ from a plain program's by a relative error of at most 0.009.
Values sent between devices are 32-bit elements; how exact they have to be, the bound alone decides.
No kernel may reach another device: no remote copies, remote signals or barrier semaphores. Data moves between devices by JAX's collectives and lax.ppermute only.
A program may use at most 192 MiB of HBM per device.

v0:
```python
import math

import jax
import jax.numpy as jnp
import numpy as np
from jax import lax
from jax.sharding import PartitionSpec as P

EPSILON = 1e-06
HIGHEST = lax.Precision.HIGHEST


def band_table(length, bands):
    highest = length / 4.0
    return np.array(
        [math.floor(highest ** (number / (bands - 1)) + 0.5) for number in range(bands)], np.int32
    )


def embedding(positions, length, bands):
    band_freq = jnp.asarray(band_table(length, bands)).astype(jnp.int32)
    phase = positions[None, :] * band_freq[:, None] % length
    angle = 2.0 * math.pi / length * phase.astype(jnp.float32)
    linear = (positions.astype(jnp.float32) / length)[None, :]
    return jnp.concatenate([linear, jnp.cos(angle), jnp.sin(angle)], axis=0)


def filter_rows(
    weight_in, bias_in, weight_mid, bias_mid, weight_out, decay_rate, positions, length
):
    bands = (weight_in.shape[1] - 1) // 2
    feature = embedding(positions, length, bands)
    hidden = jnp.sin(jnp.dot(weight_in, feature, precision=HIGHEST) + bias_in[:, None])
    for middle in range(2):
        hidden = jnp.sin(
            jnp.dot(weight_mid[middle], hidden, precision=HIGHEST) + bias_mid[middle][:, None]
        )
    shaped = jnp.dot(weight_out, hidden, precision=HIGHEST)
    scaled_pos = (positions.astype(jnp.float32) / length)[None, :]
    return shaped * jnp.exp(-decay_rate[:, None] * scaled_pos)


def dft_tables(length):
    total = 2 * length
    col_count = 128
    row_count = total // col_count
    row_ids = jnp.arange(row_count, dtype=jnp.int32)
    half_ids = jnp.arange(row_count // 2, dtype=jnp.int32)
    col_ids = jnp.arange(col_count, dtype=jnp.int32)
    angle_rows = (
        2.0
        * math.pi
        / row_count
        * (row_ids[:, None] * half_ids[None, :] % row_count).astype(jnp.float32)
    )
    angle_cols = (
        2.0
        * math.pi
        / col_count
        * (col_ids[:, None] * col_ids[None, :] % col_count).astype(jnp.float32)
    )
    angle_twist = (
        2.0 * math.pi / total * (row_ids[:, None] * col_ids[None, :] % total).astype(jnp.float32)
    )
    low = jnp.bfloat16
    return (
        row_count,
        col_count,
        total,
        jnp.cos(angle_rows).astype(low),
        jnp.sin(angle_rows).astype(low),
        jnp.cos(angle_cols).astype(low),
        jnp.sin(angle_cols).astype(low),
        jnp.cos(angle_twist),
        jnp.sin(angle_twist),
    )


def forward(signal, tables):
    row_count, col_count, total, cos_rows, sin_rows, cos_cols, sin_cols, cos_twist, sin_twist = (
        tables
    )
    shaped = signal.reshape(signal.shape[:-1] + (row_count // 2, col_count)).astype(jnp.bfloat16)
    first_re = jnp.einsum("ka,...ab->...kb", cos_rows, shaped, preferred_element_type=jnp.float32)
    first_im = -jnp.einsum("ka,...ab->...kb", sin_rows, shaped, preferred_element_type=jnp.float32)
    twist_re = (first_re * cos_twist + first_im * sin_twist).astype(jnp.bfloat16)
    twist_im = (first_im * cos_twist - first_re * sin_twist).astype(jnp.bfloat16)
    spec_re = jnp.einsum(
        "...kb,bq->...kq", twist_re, cos_cols, preferred_element_type=jnp.float32
    ) + jnp.einsum("...kb,bq->...kq", twist_im, sin_cols, preferred_element_type=jnp.float32)
    spec_im = jnp.einsum(
        "...kb,bq->...kq", twist_im, cos_cols, preferred_element_type=jnp.float32
    ) - jnp.einsum("...kb,bq->...kq", twist_re, sin_cols, preferred_element_type=jnp.float32)
    return (spec_re, spec_im)


def inverse(spec_re, spec_im, tables):
    row_count, col_count, total, cos_rows, sin_rows, cos_cols, sin_cols, cos_twist, sin_twist = (
        tables
    )
    part_re = spec_re.astype(jnp.bfloat16)
    part_im = spec_im.astype(jnp.bfloat16)
    back_re = jnp.einsum(
        "...kq,qb->...kb", part_re, cos_cols, preferred_element_type=jnp.float32
    ) - jnp.einsum("...kq,qb->...kb", part_im, sin_cols, preferred_element_type=jnp.float32)
    back_im = jnp.einsum(
        "...kq,qb->...kb", part_re, sin_cols, preferred_element_type=jnp.float32
    ) + jnp.einsum("...kq,qb->...kb", part_im, cos_cols, preferred_element_type=jnp.float32)
    turn_re = (back_re * cos_twist - back_im * sin_twist).astype(jnp.bfloat16)
    turn_im = (back_re * sin_twist + back_im * cos_twist).astype(jnp.bfloat16)
    signal = jnp.einsum(
        "ka,...kb->...ab", cos_rows, turn_re, preferred_element_type=jnp.float32
    ) - jnp.einsum("ka,...kb->...ab", sin_rows, turn_im, preferred_element_type=jnp.float32)
    return signal.reshape(signal.shape[:-2] + (total // 2,)) / total


def local(
    value,
    gate_in,
    gate_out,
    cotangent,
    skip_gain,
    weight_in,
    bias_in,
    weight_mid,
    bias_mid,
    weight_out,
    decay_rate,
):
    length = value.shape[-1]
    chan_count = lax.axis_size("chan")
    seq_count = lax.axis_size("seq")
    block_len = length // (chan_count * seq_count)
    owner = lax.axis_index("chan") * seq_count + lax.axis_index("seq")
    positions = owner * block_len + jnp.arange(block_len, dtype=jnp.int32)

    def block_filter(wgt_in, bia_in, wgt_mid, bia_mid, wgt_out, rates):
        return filter_rows(wgt_in, bia_in, wgt_mid, bia_mid, wgt_out, rates, positions, length)

    raw_block, pullback = jax.vjp(
        block_filter, weight_in, bias_in, weight_mid, bias_mid, weight_out, decay_rate
    )
    wider = lax.all_gather(raw_block, "seq", axis=1, tiled=True)
    kernel_raw = lax.all_to_all(wider, "chan", split_axis=0, concat_axis=1, tiled=True)
    norm_value = jnp.sqrt(jnp.sum(kernel_raw * kernel_raw, axis=-1, keepdims=True) + EPSILON)
    kernel = kernel_raw / norm_value
    tables = dft_tables(length)
    kernel_re, kernel_im = forward(kernel, tables)
    val_f = value.astype(jnp.float32)
    gin_f = gate_in.astype(jnp.float32)
    gout_f = gate_out.astype(jnp.float32)
    cot_f = cotangent.astype(jnp.float32)
    mixed = gin_f * val_f
    mixed_re, mixed_im = forward(mixed, tables)
    conv_re = mixed_re * kernel_re - mixed_im * kernel_im
    conv_im = mixed_re * kernel_im + mixed_im * kernel_re
    inner = inverse(conv_re, conv_im, tables) + skip_gain[:, None] * mixed
    grad_out = (cot_f * inner).astype(jnp.bfloat16)
    grad_inner = cot_f * gout_f
    inner_re, inner_im = forward(grad_inner, tables)
    back_re = inner_re * kernel_re + inner_im * kernel_im
    back_im = inner_im * kernel_re - inner_re * kernel_im
    grad_mixed = inverse(back_re, back_im, tables) + skip_gain[:, None] * grad_inner
    grad_val = (grad_mixed * gin_f).astype(jnp.bfloat16)
    grad_gin = (grad_mixed * val_f).astype(jnp.bfloat16)
    cross_re = mixed_re * inner_re + mixed_im * inner_im
    cross_im = mixed_re * inner_im - mixed_im * inner_re
    grad_kernel = jnp.sum(inverse(cross_re, cross_im, tables), axis=0)
    skip_part = jnp.sum(grad_inner * mixed, axis=(0, 2))
    along = jnp.sum(kernel_raw * grad_kernel, axis=-1, keepdims=True)
    grad_raw = grad_kernel / norm_value - kernel_raw * along / (
        norm_value * norm_value * norm_value
    )
    spread = lax.all_to_all(grad_raw, "chan", split_axis=1, concat_axis=0, tiled=True)
    grad_block = lax.psum_scatter(spread, "seq", scatter_dimension=1, tiled=True)
    grads = pullback(grad_block)
    totals = lax.psum((grads[0], grads[1], grads[2], grads[3], grads[4], grads[5]), ("chan", "seq"))
    skip_total = lax.psum(skip_part, "seq")
    factor = 1.0 / math.sqrt(value.shape[0] * seq_count * length)
    return (
        grad_val,
        grad_gin,
        grad_out,
        skip_total * factor,
        totals[0] * factor,
        totals[1] * factor,
        totals[2] * factor,
        totals[3] * factor,
        totals[4] * factor,
        totals[5] * factor,
    )


def solution(mesh):
    return jax.shard_map(
        local,
        mesh=mesh,
        in_specs=(
            P("seq", "chan", None),
            P("seq", "chan", None),
            P("seq", "chan", None),
            P("seq", "chan", None),
            P("chan"),
            P(),
            P(),
            P(),
            P(),
            P(),
            P(),
        ),
        out_specs=(
            P("seq", "chan", None),
            P("seq", "chan", None),
            P("seq", "chan", None),
            P("chan"),
            P(),
            P(),
            P(),
            P(),
            P(),
            P(),
        ),
        check_vma=False,
    )
```

profile of v0, /device:TPU:0, one launch (start us, length us, event | category | flops | bytes accessed | tf_op | source)
XLA Modules:
  0.0 517.3 jit_solution(13547496119771512025)
XLA Ops:
  24.9 6.2 %fusion.47 = f32[2,16,128,512]{3,2,1,0:T(8,128)} fusion(bf16[2,16,256,128]{3,2,1,0:T(8,128)(2,1)S(1)} %bitcast.264), kind=kOutput, calls=%fused_computation.87 | convolution fusion | flops 1075707904 | bytes 10485760 | tf_op jit(solution)/shard_map/ka,...ab->...kb/dot_general | solution.py:85
  32.1 6.0 %fusion.51 = f32[2,16,128,512]{3,2,1,0:T(8,128)} fusion(bf16[2,16,256,128]{3,2,1,0:T(8,128)(2,1)S(1)} %bitcast.266), kind=kOutput, calls=%fused_computation.91 | convolution fusion | flops 1075707904 | bytes 10485760 | tf_op jit(solution)/shard_map/ka,...ab->...kb/dot_general | solution.py:85
  38.1 5.8 %fusion.53 = f32[2,16,128,512]{3,2,1,0:T(8,128)} fusion(bf16[2,16,256,128]{3,2,1,0:T(8,128)(2,1)S(1)} %bitcast.267), kind=kOutput, calls=%fused_computation.93 | convolution fusion | flops 1075707904 | bytes 10485760 | tf_op jit(solution)/shard_map/ka,...ab->...kb/dot_general | solution.py:84
  43.9 15.2 %fusion.1 = (bf16[2,16,512,128]{2,3,1,0:T(8,128)(2,1)}, bf16[2,16,512,128]{2,3,1,0:T(8,128)(2,1)}, bf16[2,16,512,128]{2,3,1,0:T(8,128)(2,1)}, bf16[2,16,512,128]{2,3,1,0:T(8,128)(2,1)}) fusion(f32[2,16,128,512]{3,2,1,0:T(8,128)} %fusion.47, f32[512,128]{0,1:T(8,128)S(1)} %get-tuple-element.59, f32[512,128]{0,1:T(8,128)S(1)} %get-tuple-element.60, ...), kind=kOutput, calls=%fused_computation.3 | convolution fusion | flops 1113456640 | bytes 44564480 | tf_op jit(solution)/shard_map/ka,...ab->...kb/dot_general | solution.py:84
  59.1 3.9 fusion.134
  64.5 4.8 convolution_subtract_fusion.1
  71.4 4.8 fusion.126
  76.2 4.8 convolution_add_fusion
  81.0 4.8 convolution_add_fusion.1
  85.8 20.1 %subtract_convert_fusion.1 = (bf16[2,16,512,128]{3,2,1,0:T(8,128)(2,1)}, bf16[2,16,512,128]{3,2,1,0:T(8,128)(2,1)}, f32[2,16,512,128]{3,2,1,0:T(8,128)}) fusion(f32[2,16,512,128]{3,2,1,0:T(8,128)} %convolution_add_fusion.1, f32[2,16,512,128]{3,2,1,0:T(8,128)} %convolution_add_fusion, f32[2,16,512,128]{3,2,1,0:T(8,128)} %convolution_subtract_fusion.1, ...), kind=kOutput, calls=%fused_computation.18 | convolution fusion | flops 555991040 | bytes 54525952 | tf_op jit(solution)/shard_map/...kb,bq->...kq/dot_general | solution.py:93
  105.9 7.1 %fusion.104 = f32[2,16,512,128]{2,3,1,0:T(8,128)} fusion(bf16[2,16,512,128]{3,2,1,0:T(8,128)(2,1)} %get-tuple-element.18), kind=kOutput, calls=%fused_computation.177 | convolution fusion | flops 537116672 | bytes 12582912 | tf_op jit(solution)/shard_map/...kq,qb->...kb/dot_general | solution.py:105
  113.0 4.8 fusion.118
  117.8 4.8 fusion.102
  122.6 4.8 fusion.120
  127.3 2.9 copy.91
  130.2 5.2 %all-to-all-start = ((f32[8,16,4096]{2,1,0:T(8,128)}), f32[8,16,4096]{2,1,0:T(8,128)S(1)}, u32[]{:S(2)}, u32[]{:S(2)}) async-start(f32[8,16,4096]{2,1,0:T(8,128)} %bitcast.272), calls=%async_computation | async-start | bytes 4194304 | tf_op jit(solution)/shard_map/all_to_all | solution.py:144
  135.4 13.4 %fusion.15 = f32[2,16,128,256]{3,2,1,0:T(8,128)S(1)} fusion(f32[512,128]{0,1:T(8,128)S(1)} %get-tuple-element.59, f32[512,128]{0,1:T(8,128)S(1)} %get-tuple-element.60, f32[2,16,512,128]{2,3,1,0:T(8,128)} %fusion.102, f32[2,16,512,128]{2,3,1,0:T(8,128)} %fusion.118, f32[2,16,512,128]{2,3,1,0:T(8,128)} %fusion.120, f32[2,16,512,128]{2,3,1,0:T(8,128)} %fusion.104), kind=kOutput, calls=%fused_computation.40 | convolution fusion | flops 1088290816 | bytes 38273024 | tf_op jit(solution)/shard_map/ka,...kb->...ab/dot_general | solution.py:111
  148.8 15.5 %multiply_reduce_fusion = f32[16,128,256]{2,1,0:T(8,128)} fusion(f32[2,16,128,256]{3,2,1,0:T(8,128)S(1)} %fusion.15, f32[512,128]{0,1:T(8,128)S(1)} %get-tuple-element.59, f32[512,128]{0,1:T(8,128)S(1)} %get-tuple-element.60, f32[2,16,512,128]{2,3,1,0:T(8,128)} %fusion.102, f32[2,16,512,128]{2,3,1,0:T(8,128)} %fusion.118, f32[2,16,512,128]{2,3,1,0:T(8,128)} %fusion.120, ...), kind=kOutput, calls=%fused_computation.50 | convolution fusion | flops 1090912256 | bytes 40370176 | tf_op jit(solution)/shard_map/ka,...kb->...ab/dot_general | solution.py:113
  164.3 2.9 copy.121
  167.2 2.8 reduce_sum.96
  170.0 2.9 multiply_reduce_fusion.2
  178.1 4.7 fusion.79
  182.8 4.1 fusion.18
  188.9 3.1 convolution_add_fusion.2
  192.0 3.2 convolution_subtract_fusion.2
  197.0 15.3 %add_convert_fusion.3 = (bf16[2,16,512,128]{3,2,1,0:T(8,128)(2,1)}, bf16[2,16,512,128]{3,2,1,0:T(8,128)(2,1)}, bf16[2,16,512,128]{3,2,1,0:T(8,128)(2,1)}, bf16[2,16,512,128]{3,2,1,0:T(8,128)(2,1)}) fusion(f32[2,16,512,128]{3,2,1,0:T(8,128)} %get-tuple-element.52, f32[2,16,512,128]{3,2,1,0:T(8,128)S(1)} %bitcast.262, ...), kind=kLoop, calls=%fused_computation.22 | loop fusion | flops 33554432 | bytes 58720256 | tf_op jit(solution)/shard_map/convert_element_type | solution.py:102
  212.3 7.1 %fusion.108 = f32[2,16,512,128]{2,3,1,0:T(8,128)} fusion(bf16[2,16,512,128]{3,2,1,0:T(8,128)(2,1)} %get-tuple-element.20), kind=kOutput, calls=%fused_computation.181 | convolution fusion | flops 537116672 | bytes 12582912 | tf_op jit(solution)/shard_map/...kq,qb->...kb/dot_general | solution.py:105
  219.4 4.8 fusion.122
  224.2 4.8 fusion.106
  228.9 4.8 fusion.124
  233.7 4.8 fusion.114
  238.5 4.8 fusion.130
  243.3 2.8 divide_subtract_fusion
  246.1 4.2 all-to-all-start.1
  250.3 13.7 %fusion.13 = f32[2,16,128,256]{3,2,1,0:T(8,128)S(1)} fusion(f32[512,128]{0,1:T(8,128)S(1)} %get-tuple-element.59, f32[512,128]{0,1:T(8,128)S(1)} %get-tuple-element.60, f32[2,16,512,128]{2,3,1,0:T(8,128)} %fusion.106, f32[2,16,512,128]{2,3,1,0:T(8,128)} %fusion.122, f32[2,16,512,128]{2,3,1,0:T(8,128)} %fusion.124, f32[2,16,512,128]{2,3,1,0:T(8,128)} %fusion.108), kind=kOutput, calls=%fused_computation.38 | convolution fusion | flops 1088290816 | bytes 38273024 | tf_op jit(solution)/shard_map/ka,...kb->...ab/dot_general | solution.py:111
  264.0 4.8 fusion.112
  268.8 15.5 %multiply_bitcast_fusion = f32[2,16,256,128]{2,3,1,0:T(8,128)} fusion(f32[2,16,128,256]{3,2,1,0:T(8,128)S(1)} %fusion.13, f32[512,128]{0,1:T(8,128)S(1)} %get-tuple-element.59, f32[512,128]{0,1:T(8,128)S(1)} %get-tuple-element.60, f32[2,16,512,128]{2,3,1,0:T(8,128)} %fusion.106, f32[2,16,512,128]{2,3,1,0:T(8,128)} %fusion.122, ...), kind=kOutput, calls=%fused_computation.52 | convolution fusion | flops 1090387968 | bytes 42467328 | tf_op jit(solution)/shard_map/ka,...kb->...ab/dot_general | solution.py:113
  286.3 7.0 %fusion.132 = f32[2,16,512,128]{2,3,1,0:T(8,128)} fusion(bf16[2,16,512,128]{3,2,1,0:T(8,128)(2,1)} %get-tuple-element.33), kind=kOutput, calls=%fused_computation.205 | convolution fusion | flops 537116672 | bytes 12582912 | tf_op jit(solution)/shard_map/...kq,qb->...kb/dot_general | solution.py:103
  293.2 5.8 %copy.116 = f32[2,16,256,128]{3,2,1,0:T(8,128)} copy(f32[2,16,256,128]{2,3,1,0:T(8,128)} %multiply_bitcast_fusion) | data formatting | bytes 8388608 | tf_op jit(solution)/shard_map/div | solution.py:114
  299.0 5.0 div.59
  304.0 13.5 %fusion.11 = f32[2,16,128,256]{3,2,1,0:T(8,128)S(1)} fusion(f32[512,128]{0,1:T(8,128)S(1)} %get-tuple-element.59, f32[512,128]{0,1:T(8,128)S(1)} %get-tuple-element.60, f32[2,16,512,128]{2,3,1,0:T(8,128)} %fusion.112, f32[2,16,512,128]{2,3,1,0:T(8,128)} %fusion.130, f32[2,16,512,128]{2,3,1,0:T(8,128)} %fusion.132, f32[2,16,512,128]{2,3,1,0:T(8,128)} %fusion.114), kind=kOutput, calls=%fused_computation.36 | convolution fusion | flops 1088290816 | bytes 38273024 | tf_op jit(solution)/shard_map/ka,...kb->...ab/dot_general | solution.py:111
  317.5 15.7 %multiply_bitcast_fusion.1 = f32[2,16,256,128]{2,3,1,0:T(8,128)} fusion(f32[2,16,128,256]{3,2,1,0:T(8,128)S(1)} %fusion.11, f32[512,128]{0,1:T(8,128)S(1)} %get-tuple-element.59, f32[512,128]{0,1:T(8,128)S(1)} %get-tuple-element.60, f32[2,16,512,128]{2,3,1,0:T(8,128)} %fusion.112, f32[2,16,512,128]{2,3,1,0:T(8,128)} %fusion.130, ...), kind=kOutput, calls=%fused_computation.54 | convolution fusion | flops 1090387968 | bytes 42467328 | tf_op jit(solution)/shard_map/ka,...kb->...ab/dot_general | solution.py:113
  333.2 5.3 %copy.105 = f32[2,16,256,128]{3,2,1,0:T(8,128)} copy(f32[2,16,256,128]{2,3,1,0:T(8,128)} %multiply_bitcast_fusion.1) | data formatting | bytes 8388608 | tf_op jit(solution)/shard_map/div | solution.py:114
  338.6 5.2 div.56
  343.8 8.7 %fusion.10 = (bf16[2,16,32768]{2,1,0:T(8,128)(2,1)}, bf16[2,16,32768]{2,1,0:T(8,128)(2,1)}, f32[16]{0:T(128)S(1)}, bf16[2,16,32768]{2,1,0:T(8,128)(2,1)}) fusion(bf16[2,16,32768]{2,1,0:T(8,128)(2,1)S(1)} %copy-done.13, f32[2,16,32768]{2,1,0:T(8,128)} %div.56, bf16[2,16,32768]{2,1,0:T(8,128)(2,1)} %param.14, bf16[2,16,32768]{2,1,0:T(8,128)(2,1)} %param.15, ...), kind=kLoop, calls=%fused_computation.35 | loop fusion | flops 18874352 | bytes 23068800 | tf_op jit(solution)/shard_map/convert_element_type | solution.py:165
  352.6 12.4 %psum.49 = f32[16]{0:T(128)S(1)} all-reduce(f32[16]{0:T(128)S(1)} %get-tuple-element.32), channel_id=1, replica_groups=mesh['chan'=8,'seq'=4] {'seq'}, use_global_device_ids=true, to_apply=%region_2.3 | all-reduce | flops 16 | bytes 128 | tf_op jit(solution)/shard_map/psum | solution.py:178
  366.8 2.7 fusion.305
  378.3 124.6 %all-reduce.7.cloned.1.call-done = (f32[64,33]{0,1:T(8,128)}, f32[64]{0:T(128)}, f32[2,64,64]{2,1,0:T(8,128)}, f32[2,64]{1,0:T(2,128)}, f32[128,64]{0,1:T(8,128)}, /*index=5*/f32[128]{0:T(128)}) async-done(((f32[64,33]{0,1:T(8,128)}, f32[64]{0:T(128)}, f32[2,64,64]{2,1,0:T(8,128)}, f32[2,64]{1,0:T(2,128)}, f32[128,64]{0,1:T(8,128)}, /*index=5*/f32[128]{0:T(128)}), (f32[64,33]{0,1:T(8,128)}, f32[64]{0:T(128)}, ...) | async-done | bytes 75280 | tf_op jit(solution)/shard_map/psum | solution.py:177
  (138 shorter events, 51.3 us)
Async XLA Ops:
  7.2 12.1 %copy-start = (f32[128,64]{0,1:T(8,128)S(1)}, f32[128,64]{0,1:T(8,128)}, u32[]{:S(2)}) copy-start(f32[128,64]{0,1:T(8,128)} %param.21) | copy-start | bytes 98308
  7.2 15.1 %copy-start.12 = (bf16[2,16,32768]{2,1,0:T(8,128)(2,1)S(1)}, bf16[2,16,32768]{2,1,0:T(8,128)(2,1)}, u32[]{:S(2)}) copy-start(bf16[2,16,32768]{2,1,0:T(8,128)(2,1)} %param.12) | copy-start | bytes 6291460
  7.2 120.1 %all-gather.2.cloned.1.call-start = ((), (), s32[]{:S(2)}) async-start(), calls=%async_computation.3 | async-start | bytes 2621440 | tf_op jit(solution)/shard_map/all_gather | solution.py:143
  7.3 5.2 %copy-start.34 = (f32[1,1024]{1,0:T(1,128)}, f32[1,1024]{1,0:T(1,128)S(1)}, u32[]{:S(2)}) copy-start(f32[1,1024]{1,0:T(1,128)S(1)} %convert_multiply_fusion.6) | copy-start | bytes 12292
  7.3 13.9 %copy-start.32 = (f32[1024]{0:T(1024)}, f32[1024]{0:T(1024)S(1)}, u32[]{:S(2)}) copy-start(f32[1024]{0:T(1024)S(1)} %convert_multiply_fusion.5) | copy-start | bytes 12292
  8.8 12.4 %copy-start.36 = (f32[128]{0:T(128)}, f32[128]{0:T(128)S(1)}, u32[]{:S(2)}) copy-start(f32[128]{0:T(128)S(1)} %neg.30) | copy-start | bytes 1540
  9.8 2.7 copy-start.27
  9.8 2.7 copy-start.29
  12.5 2.7 copy-start.19
  15.2 0.7 copy-start.21
  18.5 0.7 copy-start.17
  24.9 6.2 %copy-start.14 = (bf16[2,16,32768]{2,1,0:T(8,128)(2,1)S(1)}, bf16[2,16,32768]{2,1,0:T(8,128)(2,1)}, u32[]{:S(2)}) copy-start(bf16[2,16,32768]{2,1,0:T(8,128)(2,1)} %param.14) | copy-start | bytes 6291460
  24.9 6.2 %copy-start.15 = (bf16[2,16,32768]{2,1,0:T(8,128)(2,1)S(1)}, bf16[2,16,32768]{2,1,0:T(8,128)(2,1)}, u32[]{:S(2)}) copy-start(bf16[2,16,32768]{2,1,0:T(8,128)(2,1)} %param.15) | copy-start | bytes 6291460
  59.1 3.9 copy-start.7
  64.4 4.8 copy-start.10
  69.2 2.2 copy-start.6
  76.2 4.8 copy-start.5
  105.9 7.1 %copy-start.9 = (bf16[2,16,512,128]{3,2,1,0:T(8,128)(2,1)S(1)}, bf16[2,16,512,128]{3,2,1,0:T(8,128)(2,1)}, u32[]{:S(2)}) copy-start(bf16[2,16,512,128]{3,2,1,0:T(8,128)(2,1)} %get-tuple-element.18) | copy-start | bytes 12582916
  113.0 4.8 copy-start.8
  130.2 39.8 %all-to-all-start = ((f32[8,16,4096]{2,1,0:T(8,128)}), f32[8,16,4096]{2,1,0:T(8,128)S(1)}, u32[]{:S(2)}, u32[]{:S(2)}) async-start(f32[8,16,4096]{2,1,0:T(8,128)} %bitcast.272), calls=%async_computation | async-start | bytes 4194304 | tf_op jit(solution)/shard_map/all_to_all | solution.py:144
  178.1 4.7 copy-start.24
  187.9 7.3 %slice-start.2 = ((s8[8388608]{0:T(1024)(128)(4,1)}), s8[4194304]{0:T(1024)(128)(4,1)S(1)}, s32[]{:S(2)}) async-start(s8[8388608]{0:T(1024)(128)(4,1)} %bitcast.261), calls=%async_computation.8 | async-start | bytes 8388608
  188.9 6.3 %slice-start = ((s8[8388608]{0:T(1024)(128)(4,1)}), s8[4194304]{0:T(1024)(128)(4,1)S(1)}, s32[]{:S(2)}) async-start(s8[8388608]{0:T(1024)(128)(4,1)} %bitcast.259), calls=%async_computation.6 | async-start | bytes 8388608
  188.9 6.3 %slice-start.3 = ((s8[8388608]{0:T(1024)(128)(4,1)}), s8[4194304]{0:T(1024)(128)(4,1)S(1)}, s32[]{:S(2)}) async-start(s8[8388608]{0:T(1024)(128)(4,1)} %bitcast.261), calls=%async_computation.9 | async-start | bytes 8388608
  192.0 4.9 slice-start.1
  212.3 7.1 %copy-start.4 = (bf16[2,16,512,128]{3,2,1,0:T(8,128)(2,1)S(1)}, bf16[2,16,512,128]{3,2,1,0:T(8,128)(2,1)}, u32[]{:S(2)}) copy-start(bf16[2,16,512,128]{3,2,1,0:T(8,128)(2,1)} %get-tuple-element.20) | copy-start | bytes 12582916
  219.4 4.8 copy-start.3
  228.9 4.8 copy-start.2
  238.5 4.8 copy-start.11
  246.1 38.3 %all-to-all-start.1 = ((f32[16,8,4096]{2,0,1:T(8,128)}), f32[16,8,4096]{2,0,1:T(8,128)S(1)}, u32[]{:S(2)}, u32[]{:S(2)}) async-start(f32[16,8,4096]{2,0,1:T(8,128)} %divide_subtract_fusion), calls=%async_computation.1 | async-start | bytes 4194304 | tf_op jit(solution)/shard_map/all_to_all | solution.py:174
  250.3 114.7 %reduce-scatter.2.cloned.1.call-start = ((), (), s32[]{:S(2)}) async-start(), calls=%async_computation.4 | async-start | bytes 2621440 | tf_op jit(solution)/shard_map/reduce_scatter | solution.py:175
  250.3 13.7 %copy-start.1 = (bf16[2,16,512,128]{3,2,1,0:T(8,128)(2,1)S(1)}, bf16[2,16,512,128]{3,2,1,0:T(8,128)(2,1)}, u32[]{:S(2)}) copy-start(bf16[2,16,512,128]{3,2,1,0:T(8,128)(2,1)} %get-tuple-element.33) | copy-start | bytes 12582916
  286.2 216.6 %all-reduce.7.cloned.1.call-start = ((), (), s32[]{:S(2)}) async-start(), calls=%async_computation.5 | async-start | bytes 241664 | tf_op jit(solution)/shard_map/psum | solution.py:177
  338.6 5.2 copy-start.13
  338.6 5.2 copy-start.38
  343.7 21.2 %copy-start.23 = (f32[128,1024]{0,1:T(8,128)S(1)}, f32[128,1024]{0,1:T(8,128)}, u32[]{:S(2)}) copy-start(f32[128,1024]{0,1:T(8,128)} %get-tuple-element.51) | copy-start | bytes 1572868
  343.7 21.3 %copy-start.33 = (f32[1024]{0:T(1024)S(1)}, f32[1024]{0:T(1024)}, u32[]{:S(2)}) copy-start(f32[1024]{0:T(1024)} %copy-done.32) | copy-start | bytes 12292
  343.7 21.3 %copy-start.37 = (f32[128]{0:T(128)S(1)}, f32[128]{0:T(128)}, u32[]{:S(2)}) copy-start(f32[128]{0:T(128)} %copy-done.36) | copy-start | bytes 1540
  343.8 23.1 %copy-start.25 = (f32[1024,64]{0,1:T(8,128)S(1)}, f32[1024,64]{0,1:T(8,128)}, u32[]{:S(2)}) copy-start(f32[1024,64]{0,1:T(8,128)} %get-tuple-element.49) | copy-start | bytes 786436
  343.8 25.8 %copy-start.22 = (f32[1024,64]{0,1:T(8,128)S(1)}, f32[1024,64]{0,1:T(8,128)}, u32[]{:S(2)}) copy-start(f32[1024,64]{0,1:T(8,128)} %copy-done.21) | copy-start | bytes 786436
  343.8 26.2 %copy-start.31 = (f32[2,64,64]{2,1,0:T(8,128)S(1)}, f32[2,64,64]{2,1,0:T(8,128)}, u32[]{:S(2)}) copy-start(f32[2,64,64]{2,1,0:T(8,128)} %param.19) | copy-start | bytes 98308
  343.8 28.4 %copy-start.20 = (f32[1024,64]{0,1:T(8,128)S(1)}, f32[1024,64]{0,1:T(8,128)}, u32[]{:S(2)}) copy-start(f32[1024,64]{0,1:T(8,128)} %copy-done.19) | copy-start | bytes 786436
  352.5 20.1 %copy-start.26 = (f32[1024,64]{0,1:T(8,128)S(1)}, f32[1024,64]{0,1:T(8,128)}, u32[]{:S(2)}) copy-start(f32[1024,64]{0,1:T(8,128)} %get-tuple-element.45) | copy-start | bytes 786436
  352.5 21.8 %copy-start.28 = (f32[16,1024]{1,0:T(8,128)S(1)}, f32[16,1024]{1,0:T(8,128)}, u32[]{:S(2)}) copy-start(f32[16,1024]{1,0:T(8,128)} %copy-done.27) | copy-start | bytes 196612
  352.5 21.8 %copy-start.30 = (f32[16,1024]{1,0:T(8,128)S(1)}, f32[16,1024]{1,0:T(8,128)}, u32[]{:S(2)}) copy-start(f32[16,1024]{1,0:T(8,128)} %copy-done.29) | copy-start | bytes 196612
  352.5 21.8 %copy-start.35 = (f32[1,1024]{1,0:T(1,128)S(1)}, f32[1,1024]{1,0:T(1,128)}, u32[]{:S(2)}) copy-start(f32[1,1024]{1,0:T(1,128)} %copy-done.34) | copy-start | bytes 12292
  352.6 24.0 %copy-start.18 = (f32[1024,64]{0,1:T(8,128)S(1)}, f32[1024,64]{0,1:T(8,128)}, u32[]{:S(2)}) copy-start(f32[1024,64]{0,1:T(8,128)} %copy-done.17) | copy-start | bytes 786436
  365.0 11.6 %copy-start.16 = (f32[128,1024]{0,1:T(8,128)S(1)}, f32[128,1024]{0,1:T(8,128)}, u32[]{:S(2)}) copy-start(f32[128,1024]{0,1:T(8,128)} %reduce-scatter.2.cloned.1.call-done) | copy-start | bytes 1572868
Sparse Core Ops, SparseCore 0:
  21.4 48.3 all-gather.1
  286.3 45.2 reduce-scatter.1
  377.9 124.9 all-reduce.6
where the time goes:
time: 524 us; the launch traced here: 517 us
  matrix products  267 us (51%)
  waiting for transfers between devices  125 us (24%)
  other arithmetic  46.2 us (9%)
  local copies, waits for them, and re-layouts  42.7 us (8%)
  between operations  14.6 us (3%)
  blocking collectives  12.4 us (2%)
  starting transfers between devices  9.5 us (2%)
    psum x1, waiting for transfers between devices, local(): lax.psum((grads[0], grads[1], grads[2], grads[3], grads[4], grads[5]), ('...  125 us
    dot_general x3, matrix products, inverse(): jnp.einsum('ka,...kb->...ab', sin_rows, turn_im, preferred_element_type=j...  46.7 us
    dot_general x3, matrix products, inverse(): jnp.einsum('ka,...kb->...ab', cos_rows, turn_re, preferred_element_type=j...  40.6 us
    dot_general x3, matrix products, forward(): jnp.einsum('...kb,bq->...kq', twist_re, sin_cols, preferred_element_type=...  28.1 us
    dot_general x3, matrix products, forward(): jnp.einsum('ka,...ab->...kb', cos_rows, shaped, preferred_element_type=jn...  25.1 us
    div x4, local copies, waits for them, and re-layouts, inverse(): return signal.reshape(signal.shape[:-2] + (total // 2,)) / total  21.3 us
    dot_general x3, matrix products, inverse(): jnp.einsum('...kq,qb->...kb', part_im, sin_cols, preferred_element_type=j...  19 us
    dot_general x3, matrix products, forward(): jnp.einsum('ka,...ab->...kb', sin_rows, shaped, preferred_element_type=jn...  16.9 us
  transfers between devices with their start and end apart: 5, of which 1 were waited for; matrix products, arithmetic and copies ran while one was open for 46% of the time, Pallas kernels for 0%

commit v1 on v0

v1 whole, which is shorter than its diff:
```python
import functools
import math

import jax
import jax.numpy as jnp
import numpy as np
from jax import lax
from jax.experimental import pallas as pl
from jax.experimental.pallas import tpu as pltpu
from jax.sharding import PartitionSpec as P

EPSILON = 1e-06
LANES = 128
F32 = jnp.float32
LOW = jnp.bfloat16


def band_table(length, bands):
    highest = length / 4.0
    return np.array(
        [math.floor(highest ** (number / (bands - 1)) + 0.5) for number in range(bands)], np.int32
    )


def feature_tables(length, bands, rows):
    freq = np.zeros((rows, LANES), np.int32)
    shift = np.zeros((rows, LANES), np.int32)
    table = band_table(length, bands)[:, None]
    freq[1 : 1 + bands] = table
    shift[1 : 1 + bands] = length // 4
    freq[1 + bands : 1 + 2 * bands] = table
    return freq, shift


def dft_tables(length):
    half = length // LANES
    rows = 2 * half
    k = np.arange(half)[:, None]
    a = np.arange(half)[None, :]
    angle = 2.0 * np.pi / rows * (k * a % rows)
    cos_rows = np.cos(angle)
    sin_rows = np.sin(angle)
    alternating = 1.0 - 2.0 * (np.arange(half) % 2)
    first = np.concatenate([cos_rows, -sin_rows], axis=0)
    first[half] = alternating
    weight = np.full((half, 1), 2.0)
    weight[0] = 1.0
    last = np.concatenate([cos_rows * weight, -sin_rows * weight], axis=0)
    last[half] = alternating
    last = last.T / (2.0 * length)
    col = np.arange(LANES)
    angle = 2.0 * np.pi / LANES * (col[:, None] * col[None, :] % LANES)
    cos_cols, sin_cols = np.cos(angle), np.sin(angle)
    ahead = np.block([[cos_cols, -sin_cols], [sin_cols, cos_cols]])
    back = np.block([[cos_cols, sin_cols], [-sin_cols, cos_cols]])
    total = 2 * length
    twist_rows = np.arange(half + 8)[:, None]
    angle = 2.0 * np.pi / total * (twist_rows * col[None, :] % total)
    low = lambda x: x.astype(np.float32).astype(LOW)
    return (
        low(first),
        low(ahead),
        low(back),
        low(last),
        np.cos(angle).astype(np.float32),
        np.sin(angle).astype(np.float32),
    )


def forward_pair(signal, tabs, r_ref, h_ref):
    first, ahead, cos_t, sin_t = tabs
    half = signal.shape[0]
    groups = half // 8
    r_ref[...] = jnp.dot(first[...], signal, preferred_element_type=F32)
    top = lax.broadcasted_iota(jnp.int32, (8, LANES), 0) == 0
    for g in range(groups + 1):
        cosine = cos_t[8 * g : 8 * g + 8, :]
        sine = sin_t[8 * g : 8 * g + 8, :]
        real, imag = [], []
        for c in range(2):
            lanes = slice(LANES * c, LANES * c + LANES)
            if g < groups:
                g_re = r_ref[8 * g : 8 * g + 8, lanes]
                g_im = r_ref[half + 8 * g : half + 8 * g + 8, lanes]
                if g == 0:
                    g_im = jnp.where(top, 0.0, g_im)
                real.append(g_re * cosine + g_im * sine)
                imag.append(g_im * cosine - g_re * sine)
            else:
                g_re = jnp.where(top, r_ref[half : half + 8, lanes], 0.0)
                real.append(g_re * cosine)
                imag.append(-(g_re * sine))
        rows = slice(16 * g, 16 * g + 16)
        h_ref[rows, :LANES] = jnp.concatenate(real, axis=0).astype(LOW)
        h_ref[rows, LANES:] = jnp.concatenate(imag, axis=0).astype(LOW)
    return jnp.dot(h_ref[...], ahead[...], preferred_element_type=F32)


def inverse_pair(s_ref, tabs, b_ref, t_ref):
    back, last, cos_t, sin_t = tabs
    half = last.shape[0]
    groups = half // 8
    b_ref[...] = jnp.dot(s_ref[...], back[...], preferred_element_type=F32)
    top = lax.broadcasted_iota(jnp.int32, (8, LANES), 0) == 0

    def turned(g, c):
        rows = slice(16 * g + 8 * c, 16 * g + 8 * c + 8)
        re, im = b_ref[rows, :LANES], b_ref[rows, LANES:]
        cosine = cos_t[8 * g : 8 * g + 8, :]
        sine = sin_t[8 * g : 8 * g + 8, :]
        return re * cosine - im * sine, re * sine + im * cosine

    for c in range(2):
        lanes = slice(LANES * c, LANES * c + LANES)
        for g in range(0, groups, 2):
            re0, im0 = turned(g, c)
            re1, im1 = turned(g + 1, c)
            if g == 0:
                im0 = jnp.where(top, turned(groups, c)[0], im0)
            t_ref[8 * g : 8 * g + 16, lanes] = jnp.concatenate([re0, re1], axis=0).astype(LOW)
            t_ref[half + 8 * g : half + 8 * g + 16, lanes] = jnp.concatenate(
                [im0, im1], axis=0
            ).astype(LOW)
    return jnp.dot(last[...], t_ref[...], preferred_element_type=F32)


def spectra_kernel(
    base_ref, val, gin, gout, cot, first, ahead, cos_t, sin_t,
    fm_out, fg_out, cross_out, skip_out,
    mix_s, grad_s, skip_s, r0, r1, h0, h1, *, chunks, seqs, chans,
):
    step = pl.program_id(0)
    chunk_rows = val.shape[2] // LANES
    half = chunk_rows * chunks

    @pl.when(step == 0)
    def _():
        skip_s[...] = jnp.zeros_like(skip_s)

    @pl.when(step < chunks)
    def _():
        for b in range(seqs):
            total = skip_s[...]
            for a in range(chunk_rows):
                lanes = slice(LANES * a, LANES * a + LANES)
                mixed = gin[b, :, lanes].astype(F32) * val[b, :, lanes].astype(F32)
                inner = cot[b, :, lanes].astype(F32) * gout[b, :, lanes].astype(F32)
                rows = pl.ds(pl.multiple_of((step * chunk_rows + a) * chans, chans), chans)
                mix_s[b, rows, :] = mixed
                grad_s[b, rows, :] = inner
                total = total + mixed * inner
            skip_s[...] = total

    @pl.when(step == chunks - 1)
    def _():
        per_row = jnp.sum(skip_s[...], axis=1, keepdims=True)
        lane = lax.broadcasted_iota(jnp.int32, (chans, LANES), 1)
        row = lax.broadcasted_iota(jnp.int32, (chans, LANES), 0)
        mine = lane == row + base_ref[0]
        spread = jnp.sum(jnp.where(mine, per_row, 0.0), axis=0, keepdims=True)
        top = lax.broadcasted_iota(jnp.int32, (8, LANES), 0) == 0
        skip_out[...] = jnp.where(top, spread, 0.0)

    @pl.when(step >= chunks)
    def _():
        pair = step - chunks
        tabs = (first, ahead, cos_t, sin_t)
        for b in range(seqs):
            def picked(ref):
                parts = [
                    ref[b, pl.ds(2 * pair + c, half, stride=chans), :] for c in range(2)
                ]
                return jnp.concatenate(parts, axis=1).astype(LOW)

            fm_out[b, 0] = forward_pair(picked(mix_s), tabs, r0, h0)
            fg_out[b, 0] = forward_pair(picked(grad_s), tabs, r1, h1)
        for g in range(half // 8 + 1):
            rows = slice(16 * g, 16 * g + 16)
            cross_re = cross_im = None
            for b in range(seqs):
                m_re, m_im = fm_out[b, 0, rows, :LANES], fm_out[b, 0, rows, LANES:]
                g_re, g_im = fg_out[b, 0, rows, :LANES], fg_out[b, 0, rows, LANES:]
                c_re = m_re * g_re + m_im * g_im
                c_im = m_re * g_im - m_im * g_re
                cross_re = c_re if b == 0 else cross_re + c_re
                cross_im = c_im if b == 0 else cross_im + c_im
            cross_out[0, rows, :LANES] = cross_re.astype(LOW)
            cross_out[0, rows, LANES:] = cross_im.astype(LOW)


def kernel_kernel(
    base_ref, cross, raw, first, ahead, back, last, cos_t, sin_t,
    fk_out, grad_out, rate_out,
    r0, h0, b0, t0, *, length,
):
    pair = pl.program_id(0)
    blocks, _, rows_each, _ = raw.shape
    half = blocks * rows_each
    lane = lax.broadcasted_iota(jnp.int32, (8, LANES), 1)
    top = lax.broadcasted_iota(jnp.int32, (8, LANES), 0) == 0
    position = (
        lax.broadcasted_iota(jnp.int32, (half, LANES), 0) * LANES
        + lax.broadcasted_iota(jnp.int32, (half, LANES), 1)
    ).astype(F32) * (-1.0 / length)

    @pl.when(pair == 0)
    def _():
        rate_out[...] = jnp.zeros_like(rate_out)

    shaped, norms = [], []
    for c in range(2):
        row = raw[:, c].reshape(half, LANES)
        norm = jnp.sqrt(jnp.sum(row * row, keepdims=True) + EPSILON)
        norms.append(norm)
        shaped.append(row / norm)
    signal = jnp.concatenate(shaped, axis=1).astype(LOW)
    fk_out[0] = forward_pair(signal, (first, ahead, cos_t, sin_t), r0, h0)
    grads = inverse_pair(cross.at[0], (back, last, cos_t, sin_t), b0, t0)
    for c in range(2):
        row = raw[:, c].reshape(half, LANES)
        grad = grads[:, LANES * c : LANES * c + LANES]
        norm = norms[c]
        along = jnp.sum(row * grad, keepdims=True)
        grad_raw = grad / norm - row * (along / (norm * norm * norm))
        grad_out[:, c] = grad_raw.reshape(blocks, rows_each, LANES)
        rate = jnp.sum(grad_raw * row * position, keepdims=True)
        mine = jnp.logical_and(lane == base_ref[0] + 2 * pair + c, top)
        rate_out[...] = rate_out[...] + jnp.where(mine, rate, 0.0)


def output_kernel(
    fm, fg, fk, val, gin, gout, cot, skip, back, last, cos_t, sin_t,
    val_out, gin_out, gout_out,
    conv_s, corr_s, s0, s1, b0, b1, t0, t1, *, pairs, chunks, seqs, chans,
):
    step = pl.program_id(0)
    chunk_rows = val.shape[2] // LANES
    half = chunk_rows * chunks

    @pl.when(step < pairs)
    def _():
        tabs = (back, last, cos_t, sin_t)
        for b in range(seqs):
            for g in range(half // 8 + 1):
                rows = slice(16 * g, 16 * g + 16)
                k_re, k_im = fk[0, rows, :LANES], fk[0, rows, LANES:]
                m_re, m_im = fm[b, 0, rows, :LANES], fm[b, 0, rows, LANES:]
                s0[rows, :LANES] = (m_re * k_re - m_im * k_im).astype(LOW)
                s0[rows, LANES:] = (m_re * k_im + m_im * k_re).astype(LOW)
                g_re, g_im = fg[b, 0, rows, :LANES], fg[b, 0, rows, LANES:]
                s1[rows, :LANES] = (g_re * k_re + g_im * k_im).astype(LOW)
                s1[rows, LANES:] = (g_im * k_re - g_re * k_im).astype(LOW)
            conv = inverse_pair(s0, tabs, b0, t0)
            corr = inverse_pair(s1, tabs, b1, t1)
            for c in range(2):
                lanes = slice(LANES * c, LANES * c + LANES)
                conv_s[b, pl.ds(2 * step + c, half, stride=chans), :] = conv[:, lanes]
                corr_s[b, pl.ds(2 * step + c, half, stride=chans), :] = corr[:, lanes]

    @pl.when(step >= pairs)
    def _():
        chunk = step - pairs
        lane = lax.broadcasted_iota(jnp.int32, (chans, LANES), 1)
        row = lax.broadcasted_iota(jnp.int32, (chans, LANES), 0)
        gain = jnp.sum(jnp.where(lane == row, skip[0:1, :], 0.0), axis=1, keepdims=True)
        gain = jnp.broadcast_to(gain, (chans, LANES))
        for b in range(seqs):
            for a in range(chunk_rows):
                lanes = slice(LANES * a, LANES * a + LANES)
                rows = pl.ds(pl.multiple_of((chunk * chunk_rows + a) * chans, chans), chans)
                v = val[b, :, lanes].astype(F32)
                gi = gin[b, :, lanes].astype(F32)
                go = gout[b, :, lanes].astype(F32)
                co = cot[b, :, lanes].astype(F32)
                inner = conv_s[b, rows, :] + gain * (gi * v)
                grad_mixed = corr_s[b, rows, :] + gain * (co * go)
                gout_out[b, :, lanes] = (co * inner).astype(LOW)
                val_out[b, :, lanes] = (grad_mixed * gi).astype(LOW)
                gin_out[b, :, lanes] = (grad_mixed * v).astype(LOW)


INV_PI = 0.3183098861837907
PI_HIGH = 3.140625
PI_MID = 9.67502593994140625e-4
PI_LOW = 1.509957990978376432e-7


def sine_poly(r, r2):
    p = 2.7557319e-06 + r2 * -2.50507e-08
    p = -1.98412698e-04 + r2 * p
    p = 8.33333333e-03 + r2 * p
    p = -1.66666667e-01 + r2 * p
    return r + r * (r2 * p)


def cosine_poly(r2):
    p = -2.7557319e-07 + r2 * 2.0876757e-09
    p = 2.48015873e-05 + r2 * p
    p = -1.38888889e-03 + r2 * p
    p = 4.16666667e-02 + r2 * p
    p = -0.5 + r2 * p
    return 1.0 + r2 * p


def sine_cosine(z):
    turns = jnp.floor(z * INV_PI + 0.5)
    r = ((z - turns * PI_HIGH) - turns * PI_MID) - turns * PI_LOW
    sign = 1.0 - 2.0 * (turns - 2.0 * jnp.floor(turns * 0.5))
    r2 = r * r
    return sign * sine_poly(r, r2), sign * cosine_poly(r2)


def column(row, size):
    lane = lax.broadcasted_iota(jnp.int32, (size, size), 1)
    diagonal = lane == lax.broadcasted_iota(jnp.int32, (size, size), 0)
    return jnp.sum(jnp.where(diagonal, row, 0.0), axis=1, keepdims=True)


def split(x):
    high = x.astype(LOW)
    return high, (x - high.astype(F32)).astype(LOW)


def triple_dot(weight, x):
    w_high, w_low = split(weight)
    x_high, x_low = split(x)
    dot = functools.partial(jnp.dot, preferred_element_type=F32)
    return dot(w_high, x_high) + (dot(w_high, x_low) + dot(w_low, x_high))


def filter_kernel(
    start_ref, freq, shift, w_in, b_in, w_mid, b_mid, w_out, rates,
    raw_out, feat_out, act_out, cos_out, *, length,
):
    width = feat_out.shape[1]
    order = w_in.shape[0]
    start = start_ref[0] + pl.program_id(0) * width
    rows = freq.shape[0]
    position = start + lax.broadcasted_iota(jnp.int32, (rows, width), 1)
    freq_w = jnp.concatenate([freq[...]] * (width // LANES), axis=1)
    shift_w = jnp.concatenate([shift[...]] * (width // LANES), axis=1)
    quarter = length // 4
    phase = position * freq_w + shift_w + quarter
    sign = (1 - ((phase >> int(math.log2(length // 2))) & 1) * 2).astype(F32)
    angle = ((phase & (length // 2 - 1)) - quarter).astype(F32) * (2.0 * math.pi / length)
    wave = sign * sine_poly(angle, angle * angle)
    linear = lax.broadcasted_iota(jnp.int32, (rows, width), 0) == 0
    feature = jnp.where(linear, position.astype(F32) * (1.0 / length), wave)
    feat_out[...] = feature.astype(LOW)

    def layer(weight, x, bias, number):
        z = triple_dot(weight, x) + column(bias, order)
        sine, cosine = sine_cosine(z)
        act_out[order * number : order * number + order, :] = sine.astype(LOW)
        cos_out[order * number : order * number + order, :] = cosine
        return sine

    hidden = layer(w_in[...], feature, b_in[...], 0)
    hidden = layer(w_mid[0], hidden, b_mid[0:1, :], 1)
    hidden = layer(w_mid[1], hidden, b_mid[1:2, :], 2)
    shaped = triple_dot(w_out[...], hidden)
    channels = w_out.shape[0]
    rate = column(rates[...], channels) * (-1.0 / length)
    lane = lax.broadcasted_iota(jnp.int32, (channels, LANES), 1)
    for a in range(width // LANES):
        where = (start + a * LANES + lane).astype(F32)
        raw_out[:, a, :] = shaped[:, LANES * a : LANES * a + LANES] * jnp.exp(rate * where)


def nt_dot(x, y):
    return lax.dot_general(x, y, (((1,), (1,)), ((), ())), preferred_element_type=F32)


def tn_triple(weight, x):
    w_high, w_low = split(weight.T)
    x_high, x_low = split(x)
    dot = functools.partial(jnp.dot, preferred_element_type=F32)
    return dot(w_high, x_high) + (dot(w_high, x_low) + dot(w_low, x_high))


def filter_grad_kernel(
    start_ref, grad, feat, act, cosines, w_mid, w_out, rates, rate_row, skip_row,
    packed, d_out, d_mid, d_in, d_bias, *, length,
):
    step = pl.program_id(0)
    width = feat.shape[1]
    order = w_mid.shape[1]
    channels = w_out.shape[0]
    start = start_ref[0] + step * width

    @pl.when(step == 0)
    def _():
        for ref in (d_out, d_mid, d_in, d_bias):
            ref[...] = jnp.zeros_like(ref)

    rate = column(rates[...], channels) * (-1.0 / length)
    lane = lax.broadcasted_iota(jnp.int32, (channels, LANES), 1)
    parts = []
    for a in range(width // LANES):
        where = (start + a * LANES + lane).astype(F32)
        parts.append(grad[:, a, :] * jnp.exp(rate * where))
    d_shaped = jnp.concatenate(parts, axis=1)

    def part(ref, number):
        return ref[order * number : order * number + order, :]

    def bias_sum(x, number):
        total = x[:, :LANES]
        for a in range(1, width // LANES):
            total = total + x[:, LANES * a : LANES * a + LANES]
        d_bias[number] = d_bias[number] + total

    d_out[...] = d_out[...] + nt_dot(d_shaped.astype(LOW), part(act, 2))
    dz = tn_triple(w_out[...], d_shaped) * part(cosines, 2)
    bias_sum(dz, 2)
    d_mid[1] = d_mid[1] + nt_dot(dz.astype(LOW), part(act, 1))
    dz = tn_triple(w_mid[1], dz) * part(cosines, 1)
    bias_sum(dz, 1)
    d_mid[0] = d_mid[0] + nt_dot(dz.astype(LOW), part(act, 0))
    dz = tn_triple(w_mid[0], dz) * part(cosines, 0)
    bias_sum(dz, 0)
    d_in[...] = d_in[...] + nt_dot(dz.astype(LOW), feat[...])

    @pl.when(step == pl.num_programs(0) - 1)
    def _():
        packed[...] = jnp.zeros_like(packed)
        packed[:channels, :order] = d_out[...]
        base = channels
        packed[base : base + order, :order] = d_mid[0]
        packed[base + order : base + 2 * order, :order] = d_mid[1]
        base += 2 * order
        features = d_in.shape[1]
        packed[base : base + order, :features] = d_in[...]
        spot = lax.broadcasted_iota(jnp.int32, (order, LANES), 1)
        current = packed[base : base + order, :]
        for number in range(3):
            total = jnp.sum(d_bias[number], axis=1, keepdims=True)
            current = jnp.where(spot == features + number, total, current)
        packed[base : base + order, :] = current
        base += order
        packed[base : base + 8, :] = rate_row[...]
        packed[base + 8 : base + 16, :] = skip_row[...]


def unpack_kernel(pieces, w_in, b_in, w_mid, b_mid, w_out, rate, skip, *, scale, features):
    total = pieces[0]
    for number in range(1, pieces.shape[0]):
        total = total + pieces[number]
    total = total * scale
    channels, order = w_out.shape
    w_out[...] = total[:channels, :order]
    base = channels
    w_mid[0] = total[base : base + order, :order]
    w_mid[1] = total[base + order : base + 2 * order, :order]
    base += 2 * order
    block = total[base : base + order, :]
    w_in[...] = block[:, : w_in.shape[1]]
    lane = lax.broadcasted_iota(jnp.int32, (order, LANES), 1)
    row = lax.broadcasted_iota(jnp.int32, (order, LANES), 0)

    def as_row(number):
        values = jnp.sum(jnp.where(lane == features + number, block, 0.0), axis=1, keepdims=True)
        return jnp.sum(jnp.where(lane == row, values, 0.0), axis=0, keepdims=True)[:, :order]

    b_in[...] = as_row(0)
    b_mid[0:1, :] = as_row(1)
    b_mid[1:2, :] = as_row(2)
    base += order
    rate[...] = total[base : base + 1, :]
    skip[...] = total[base + 8 : base + 9, :]


def const_spec(array):
    zeros = (0,) * len(array.shape)
    return pl.BlockSpec(array.shape, lambda i: zeros)


SCALAR = pl.BlockSpec(memory_space=pltpu.SMEM)


def vmem(shape, dtype=F32):
    return pltpu.VMEM(shape, dtype)


def shape(dims, dtype=F32):
    return jax.ShapeDtypeStruct(dims, dtype)


def fan_in(x, axis):
    size = lax.axis_size(axis)
    parts = [x]
    for d in range(1, size):
        parts.append(lax.ppermute(x, axis, [(s, (s + d) % size) for s in range(size)]))
    return parts


def local(
    value, gate_in, gate_out, cotangent, skip_gain,
    weight_in, bias_in, weight_mid, bias_mid, weight_out, decay_rate,
):
    seqs, chans, length = value.shape
    channels, order = weight_out.shape
    chan_count = lax.axis_size("chan")
    seq_count = lax.axis_size("seq")
    block = length // chan_count
    block_rows = block // LANES
    half = length // LANES
    pairs = chans // 2
    spec_rows = 2 * (half + 8)
    chunks = 8
    start = (lax.axis_index("chan") * block).astype(jnp.int32).reshape(1)
    base = (lax.axis_index("chan") * chans).astype(jnp.int32).reshape(1)
    first, ahead, back, last, cos_t, sin_t = [jnp.asarray(t) for t in dft_tables(length)]
    feature_rows = 48
    bands = (weight_in.shape[1] - 1) // 2
    freq, shift = [jnp.asarray(t) for t in feature_tables(length, bands, feature_rows)]

    width = min(1024, block)
    steps = block // width
    rates = decay_rate.reshape(1, channels)
    w_in_wide = jnp.pad(weight_in, ((0, 0), (0, feature_rows - weight_in.shape[1])))
    weights = (w_in_wide, bias_in.reshape(1, order), weight_mid, bias_mid, weight_out, rates)
    raw_block, feats, acts, cosines = pl.pallas_call(
        functools.partial(filter_kernel, length=length),
        grid=(steps,),
        in_specs=[SCALAR] + [const_spec(x) for x in (freq, shift) + weights],
        out_specs=[
            pl.BlockSpec((channels, width // LANES, LANES), lambda i: (0, i, 0)),
            pl.BlockSpec((feature_rows, width), lambda i: (0, i)),
            pl.BlockSpec((3 * order, width), lambda i: (0, i)),
            pl.BlockSpec((3 * order, width), lambda i: (0, i)),
        ],
        out_shape=[
            shape((channels, block_rows, LANES)),
            shape((feature_rows, block), LOW),
            shape((3 * order, block), LOW),
            shape((3 * order, block)),
        ],
        name="filter_rows",
    )(start, freq, shift, *weights)
    raw = lax.all_to_all(
        raw_block.reshape(chan_count, chans, block_rows, LANES),
        "chan", split_axis=0, concat_axis=0, tiled=True,
    )

    chunk = length // chunks
    ahead_tabs = (first, ahead, cos_t, sin_t)
    early = lambda i: (0, 0, jnp.minimum(i, chunks - 1))
    late = lambda i: (0, jnp.maximum(i - chunks, 0), 0, 0)
    fm, fg, cross, skip_row = pl.pallas_call(
        functools.partial(spectra_kernel, chunks=chunks, seqs=seqs, chans=chans),
        grid=(chunks + pairs,),
        in_specs=[SCALAR]
        + [pl.BlockSpec((seqs, chans, chunk), early)] * 4
        + [const_spec(x) for x in ahead_tabs],
        out_specs=[
            pl.BlockSpec((seqs, 1, spec_rows, 2 * LANES), late),
            pl.BlockSpec((seqs, 1, spec_rows, 2 * LANES), late),
            pl.BlockSpec((1, spec_rows, 2 * LANES), lambda i: (jnp.maximum(i - chunks, 0), 0, 0)),
            pl.BlockSpec((8, LANES), lambda i: (0, 0)),
        ],
        out_shape=[
            shape((seqs, pairs, spec_rows, 2 * LANES)),
            shape((seqs, pairs, spec_rows, 2 * LANES)),
            shape((pairs, spec_rows, 2 * LANES), LOW),
            shape((8, LANES)),
        ],
        scratch_shapes=[
            vmem((seqs, half * chans, LANES)),
            vmem((seqs, half * chans, LANES)),
            vmem((chans, LANES)),
            vmem((2 * half, 2 * LANES)),
            vmem((2 * half, 2 * LANES)),
            vmem((spec_rows, 2 * LANES), LOW),
            vmem((spec_rows, 2 * LANES), LOW),
        ],
        name="spectra",
    )(base, value, gate_in, gate_out, cotangent, *ahead_tabs)

    tables = (first, ahead, back, last, cos_t, sin_t)
    fk, grad_raw, rate_row = pl.pallas_call(
        functools.partial(kernel_kernel, length=length),
        grid=(pairs,),
        in_specs=[
            SCALAR,
            pl.BlockSpec((1, spec_rows, 2 * LANES), lambda i: (i, 0, 0)),
            pl.BlockSpec((chan_count, 2, block_rows, LANES), lambda i: (0, i, 0, 0)),
        ]
        + [const_spec(x) for x in tables],
        out_specs=[
            pl.BlockSpec((1, spec_rows, 2 * LANES), lambda i: (i, 0, 0)),
            pl.BlockSpec((chan_count, 2, block_rows, LANES), lambda i: (0, i, 0, 0)),
            pl.BlockSpec((8, LANES), lambda i: (0, 0)),
        ],
        out_shape=[
            shape((pairs, spec_rows, 2 * LANES)),
            shape((chan_count, chans, block_rows, LANES)),
            shape((8, LANES)),
        ],
        scratch_shapes=[
            vmem((2 * half, 2 * LANES)),
            vmem((spec_rows, 2 * LANES), LOW),
            vmem((spec_rows, 2 * LANES)),
            vmem((2 * half, 2 * LANES), LOW),
        ],
        name="filter_spectrum",
    )(base, cross, raw, *tables)
    grad_block = lax.all_to_all(grad_raw, "chan", split_axis=0, concat_axis=0, tiled=True)

    skip_wide = jnp.pad(skip_gain.reshape(1, chans), ((0, 7), (0, LANES - chans)))
    back_tabs = (back, last, cos_t, sin_t)
    early4 = lambda i: (0, jnp.minimum(i, pairs - 1), 0, 0)
    late3 = lambda i: (0, 0, jnp.maximum(i - pairs, 0))
    signal_spec = pl.BlockSpec((seqs, chans, chunk), late3)
    grad_val, grad_gin, grad_gout = pl.pallas_call(
        functools.partial(output_kernel, pairs=pairs, chunks=chunks, seqs=seqs, chans=chans),
        grid=(pairs + chunks,),
        in_specs=[
            pl.BlockSpec((seqs, 1, spec_rows, 2 * LANES), early4),
            pl.BlockSpec((seqs, 1, spec_rows, 2 * LANES), early4),
            pl.BlockSpec((1, spec_rows, 2 * LANES), lambda i: (jnp.minimum(i, pairs - 1), 0, 0)),
        ]
        + [signal_spec] * 4
        + [const_spec(x) for x in (skip_wide,) + back_tabs],
        out_specs=[signal_spec] * 3,
        out_shape=[shape((seqs, chans, length), LOW)] * 3,
        scratch_shapes=[
            vmem((seqs, half * chans, LANES)),
            vmem((seqs, half * chans, LANES)),
            vmem((spec_rows, 2 * LANES), LOW),
            vmem((spec_rows, 2 * LANES), LOW),
            vmem((spec_rows, 2 * LANES)),
            vmem((spec_rows, 2 * LANES)),
            vmem((2 * half, 2 * LANES), LOW),
            vmem((2 * half, 2 * LANES), LOW),
        ],
        name="outputs",
    )(fm, fg, fk, value, gate_in, gate_out, cotangent, skip_wide, *back_tabs)

    packed_rows = channels + 3 * order + 16
    grad_in = grad_block.reshape(channels, block_rows, LANES)
    packed = pl.pallas_call(
        functools.partial(filter_grad_kernel, length=length),
        grid=(steps,),
        in_specs=[
            SCALAR,
            pl.BlockSpec((channels, width // LANES, LANES), lambda i: (0, i, 0)),
            pl.BlockSpec((feature_rows, width), lambda i: (0, i)),
            pl.BlockSpec((3 * order, width), lambda i: (0, i)),
            pl.BlockSpec((3 * order, width), lambda i: (0, i)),
        ]
        + [const_spec(x) for x in (weight_mid, weight_out, rates, rate_row, skip_row)],
        out_specs=pl.BlockSpec((packed_rows, LANES), lambda i: (0, 0)),
        out_shape=shape((packed_rows, LANES)),
        scratch_shapes=[
            vmem((channels, order)),
            vmem((2, order, order)),
            vmem((order, feature_rows)),
            vmem((3, order, LANES)),
        ],
        name="filter_gradients",
    )(start, grad_in, feats, acts, cosines, weight_mid, weight_out, rates, rate_row, skip_row)

    group = functools.reduce(jnp.add, fan_in(packed, "chan"))
    pieces = jnp.stack(fan_in(group, "seq"))
    factor = 1.0 / math.sqrt(seqs * seq_count * length)
    d_in, d_bin, d_mid, d_bmid, d_out, d_rate, d_skip = pl.pallas_call(
        functools.partial(unpack_kernel, scale=factor, features=feature_rows),
        out_shape=[
            shape(weight_in.shape),
            shape((1, order)),
            shape(weight_mid.shape),
            shape(bias_mid.shape),
            shape(weight_out.shape),
            shape((1, LANES)),
            shape((1, LANES)),
        ],
        name="unpack",
    )(pieces)
    skip_total = lax.dynamic_slice(d_skip[0], (base[0],), (chans,))
    return (
        grad_val, grad_gin, grad_gout, skip_total,
        d_in, d_bin[0], d_mid, d_bmid, d_out, d_rate[0, :channels],
    )


def solution(mesh):
    large = P("seq", "chan", None)
    return jax.shard_map(
        local,
        mesh=mesh,
        in_specs=(large,) * 4 + (P("chan"),) + (P(),) * 6,
        out_specs=(large,) * 3 + (P("chan"),) + (P(),) * 6,
        check_vma=False,
    )
```

time: 524 us -> 160 us (0.31)
  matrix products: 267 us -> 0 us
  waiting for transfers between devices: 125 us -> 20.9 us
  Pallas kernels: 0 us -> 79.3 us
  other arithmetic: 46.2 us -> 1.92 us
  local copies, waits for them, and re-layouts: 42.7 us -> 9.07 us
  blocking collectives: 12.4 us -> 30.9 us
  between operations: 14.6 us -> 0.69 us
  starting transfers between devices: 9.5 us -> 15.1 us
    dot_general x47 -> x0, matrix products: 267 us -> none  [the longest x3 46.7 us: inverse(): jnp.einsum('ka,...kb->...ab', sin_rows, turn_im, preferred_element_type=j...]
    psum x1 -> x0, waiting for transfers between devices: 125 us -> none  [local(): lax.psum((grads[0], grads[1], grads[2], grads[3], grads[4], grads[5]), ('...]
    pallas_call x0 -> x6, Pallas kernels: none -> 79.3 us  [the longest x1 27.1 us: local(): pl.pallas_call(functools.partial(output_kernel, pairs=pairs, chunks=chunk...]
    all_to_all x0 -> x1, blocking collectives: none -> 30.9 us  [local(): lax.all_to_all(grad_raw, 'chan', split_axis=0, concat_axis=0, tiled=True)]
    convert_element_type x4 -> x0, other arithmetic: 26.6 us -> none  [the longest x1 15.3 us: inverse(): part_im = spec_im.astype(jnp.bfloat16)]
    div x4 -> x0, local copies, waits for them, and re-layouts: 21.3 us -> none  [inverse(): return signal.reshape(signal.shape[:-2] + (total // 2,)) / total]
    psum x1 -> x0, blocking collectives: 12.4 us -> none  [local(): skip_total = lax.psum(skip_part, 'seq')]
    ppermute x0 -> x10, waiting for transfers between devices: none -> 11.8 us  [fan_in(): lax.ppermute(x, axis, [(s, (s + d) % size) for s in range(size)])]
  transfers between devices with their start and end apart: 5 -> 11, of which waited for: 1 -> 6; matrix products, arithmetic and copies ran while one was open for 46% -> 0% of each run, Pallas kernels for 0% -> 28%
where the time goes in v1:
time: 160 us; the launch traced here: 158 us
  Pallas kernels  79.3 us (50%)
  blocking collectives  30.9 us (19%)
  waiting for transfers between devices  20.9 us (13%)
  starting transfers between devices  15.1 us (9%)
  local copies, waits for them, and re-layouts  9.07 us (6%)
  other arithmetic  1.92 us (1%)
    all_to_all x1, blocking collectives, local(): lax.all_to_all(grad_raw, 'chan', split_axis=0, concat_axis=0, tiled=True)  30.9 us
    pallas_call x1, Pallas kernels, local(): pl.pallas_call(functools.partial(output_kernel, pairs=pairs, chunks=chunk...  27.1 us
    pallas_call x1, Pallas kernels, local(): pl.pallas_call(functools.partial(spectra_kernel, chunks=chunks, seqs=seqs...  17.5 us
    pallas_call x1, Pallas kernels, local(): pl.pallas_call(functools.partial(kernel_kernel, length=length), grid=(pai...  13.3 us
    pallas_call x1, Pallas kernels, local(): pl.pallas_call(functools.partial(filter_kernel, length=length), grid=(ste...  11.8 us
    ppermute x10, waiting for transfers between devices, fan_in(): lax.ppermute(x, axis, [(s, (s + d) % size) for s in range(size)])  11.8 us
    ppermute x10, starting transfers between devices, fan_in(): lax.ppermute(x, axis, [(s, (s + d) % size) for s in range(size)])  9.9 us
    all_to_all x1, waiting for transfers between devices, local(): lax.all_to_all(raw_block.reshape(chan_count, chans, block_rows, LANES), '...  9.1 us
  transfers between devices with their start and end apart: 11, of which 6 were waited for; matrix products, arithmetic and copies ran while one was open for 0% of the time, Pallas kernels for 28%

profile of v1, /device:TPU:0, one launch (start us, length us, event | category | flops | bytes accessed | tf_op | source)
XLA Modules:
  0.0 157.9 jit_solution(11112345197111464547)
XLA Ops:
  0.6 1.5 copy.30.w_out
  2.1 0.8 copy.29
  2.9 0.6 pad.8.w_in
  3.6 11.8 %filter_rows.1 = (f32[128,32,128]{2,1,0:T(8,128)}, bf16[48,4096]{1,0:T(8,128)(2,1)}, bf16[192,4096]{1,0:T(8,128)(2,1)}, f32[192,4096]{1,0:T(8,128)}) custom-call(s32[1]{0:T(128)} %bitcast.1.start_ref, s32[48,128]{1,0:T(8,128)} %constant.39.clone.freq, s32[48,128]{1,0:T(8,128)} %constant.40.clone.shift, f32[64,48]{1,0:T(8,128)} %pad.8.w_in, ...), custom_call_target="tpu_custom_call" | custom-call | tf_op jit(solution)/shard_map/filter_rows/pallas_call | solution.py:523
  15.4 5.2 %all-to-all-start = ((f32[8,16,32,128]{3,2,1,0:T(8,128)}), f32[8,16,32,128]{3,2,1,0:T(8,128)S(1)}, u32[]{:S(2)}, u32[]{:S(2)}) async-start(f32[8,16,32,128]{3,2,1,0:T(8,128)} %bitcast.16), calls=%async_computation | async-start | bytes 4194304 | tf_op jit(solution)/shard_map/all_to_all | solution.py:541
  20.6 17.5 %spectra.1 = (f32[2,8,528,256]{3,2,1,0:T(8,128)}, f32[2,8,528,256]{3,2,1,0:T(8,128)}, bf16[8,528,256]{2,1,0:T(8,128)(2,1)}, f32[8,128]{1,0:T(8,128)}) custom-call(s32[1]{0:T(128)} %bitcast.base_ref, bf16[2,16,32768]{2,1,0:T(8,128)(2,1)} %val.3, bf16[2,16,32768]{2,1,0:T(8,128)(2,1)} %gin.3, bf16[2,16,32768]{2,1,0:T(8,128)(2,1)} %gout.3, ...), custom_call_target="tpu_custom_call" | custom-call | tf_op jit(solution)/shard_map/spectra/pallas_call | solution.py:550
  38.1 9.1 %all-to-all-done.raw = f32[8,16,32,128]{3,2,1,0:T(8,128)S(1)} async-done(((f32[8,16,32,128]{3,2,1,0:T(8,128)}), f32[8,16,32,128]{3,2,1,0:T(8,128)S(1)}, u32[]{:S(2)}, u32[]{:S(2)}) %all-to-all-start) | async-done | bytes 2097184 | tf_op jit(solution)/shard_map/all_to_all | solution.py:541
  47.2 0.0 copy-start
  47.2 1.3 copy-done
  48.5 13.3 %filter_spectrum.1 = (f32[8,528,256]{2,1,0:T(8,128)}, f32[8,16,32,128]{3,2,1,0:T(8,128)}, f32[8,128]{1,0:T(8,128)}) custom-call(s32[1]{0:T(128)} %bitcast.base_ref, bf16[8,528,256]{2,1,0:T(8,128)(2,1)} %get-tuple-element.33.cross, f32[8,16,32,128]{3,2,1,0:T(8,128)} %copy-done, bf16[512,256]{1,0:T(8,128)(2,1)} %constant.33.clone.first, ...), custom_call_target="tpu_custom_call" | custom-call | tf_op jit(solution)/shard_map/filter_spectrum/pallas_call | solution.py:581
  61.8 30.9 %all_to_all.10 = f32[8,16,32,128]{3,2,1,0:T(8,128)} all-to-all(f32[8,16,32,128]{3,2,1,0:T(8,128)} %get-tuple-element.39), channel_id=1, replica_groups=mesh['chan'=8,'seq'=4] {'chan'}, dimensions={0} | all-to-all | bytes 4194304 | tf_op jit(solution)/shard_map/all_to_all | solution.py:608
  92.7 0.0 copy-start.1
  92.7 7.7 %filter_gradients.1 = f32[336,128]{1,0:T(8,128)} custom-call(s32[1]{0:T(128)} %bitcast.1.start_ref, f32[128,32,128]{2,1,0:T(8,128)} %bitcast.15, bf16[48,4096]{1,0:T(8,128)(2,1)} %get-tuple-element.40.feat, bf16[192,4096]{1,0:T(8,128)(2,1)} %get-tuple-element.41.act, f32[192,4096]{1,0:T(8,128)} %get-tuple-element.42.cosines, f32[2,64,64]{2,1,0:T(8,128)} %w_mid.3, ...), custom_call_target="tpu_custom_call" | custom-call | tf_op jit(solution)/shard_map/filter_gradients/pallas_call | solution.py:642
  100.4 0.0 collective-permute-start
  100.4 0.6 collective-permute-start.1
  101.0 1.4 collective-permute-start.2
  102.4 1.4 collective-permute-start.3
  103.8 0.0 collective-permute-start.4
  103.8 3.8 %collective-permute-done = f32[336,128]{1,0:T(8,128)S(1)} collective-permute-done((f32[336,128]{1,0:T(8,128)}, f32[336,128]{1,0:T(8,128)S(1)}, u32[]{:S(2)}, u32[]{:S(2)}) %collective-permute-start) | collective-permute-done | bytes 172064 | tf_op jit(solution)/shard_map/ppermute | solution.py:493
  107.6 0.0 collective-permute-start.5
  107.6 1.2 collective-permute-done.1
  108.9 1.8 %collective-permute-start.6 = (f32[336,128]{1,0:T(8,128)}, f32[336,128]{1,0:T(8,128)S(1)}, u32[]{:S(2)}, u32[]{:S(2)}) collective-permute-start(f32[336,128]{1,0:T(8,128)} %filter_gradients.1), channel_id=1, source_target_pairs={{0,28},{4,0},{8,4},{12,8},{16,12},{20,16},{24,20},{28,24},{1,29},{... | collective-permute-start | bytes 516104 | tf_op jit(solution)/shard_map/ppermute | solution.py:493
  110.6 4.8 %collective-permute-done.2 = f32[336,128]{1,0:T(8,128)S(1)} collective-permute-done((f32[336,128]{1,0:T(8,128)}, f32[336,128]{1,0:T(8,128)S(1)}, u32[]{:S(2)}, u32[]{:S(2)}) %collective-permute-start.2) | collective-permute-done | bytes 172064 | tf_op jit(solution)/shard_map/ppermute | solution.py:493
  115.4 0.2 collective-permute-done.3
  115.6 1.8 %collective-permute-done.4 = f32[336,128]{1,0:T(8,128)S(1)} collective-permute-done((f32[336,128]{1,0:T(8,128)}, f32[336,128]{1,0:T(8,128)S(1)}, u32[]{:S(2)}, u32[]{:S(2)}) %collective-permute-start.4) | collective-permute-done | bytes 172064 | tf_op jit(solution)/shard_map/ppermute | solution.py:493
  117.4 0.0 collective-permute-done.5
  117.4 0.0 collective-permute-done.6
  117.4 1.0 add_add_fusion
  118.4 3.7 %collective-permute-start.9 = (f32[336,128]{1,0:T(8,128)S(1)}, f32[336,128]{1,0:T(8,128)S(1)}, u32[]{:S(2)}, u32[]{:S(2)}) collective-permute-start(f32[336,128]{1,0:T(8,128)S(1)} %add_add_fusion), channel_id=1, source_target_pairs={{0,3},{1,0},{2,1},{3,2},{4,7},{5,4},{6,5},{7,6},{8,11},{9,8},{10,9... | collective-permute-start | bytes 516104 | tf_op jit(solution)/shard_map/ppermute | solution.py:493
  122.1 0.0 collective-permute-start.7
  122.1 1.0 collective-permute-start.8
  123.1 0.0 copy-done.1
  123.1 0.6 pad.9.skip
  123.7 27.1 %outputs.1 = (bf16[2,16,32768]{2,1,0:T(8,128)(2,1)}, bf16[2,16,32768]{2,1,0:T(8,128)(2,1)}, bf16[2,16,32768]{2,1,0:T(8,128)(2,1)}) custom-call(f32[2,8,528,256]{3,2,1,0:T(8,128)} %get-tuple-element.31.fm, f32[2,8,528,256]{3,2,1,0:T(8,128)} %get-tuple-element.32.fg, f32[8,528,256]{2,1,0:T(8,128)} %get-tuple-element.35.fk, bf16[2,16,32768]{2,1,0:T(8,128)(2,1)} %val.3, ...), custom_call_target="tpu_custom_call" | custom-call | tf_op jit(solution)/shard_map/outputs/pallas_call | solution.py:615
  150.8 0.0 collective-permute-done.9
  150.8 0.0 collective-permute-done.7
  150.8 0.0 collective-permute-done.8
  150.9 0.9 pad_maximum_fusion.pieces
  151.8 1.9 %unpack.1 = (f32[64,33]{1,0:T(8,128)}, f32[1,64]{1,0:T(1,128)}, f32[2,64,64]{2,1,0:T(8,128)}, f32[2,64]{1,0:T(2,128)}, f32[128,64]{1,0:T(8,128)}, /*index=5*/f32[1,128]{1,0:T(1,128)}, f32[1,128]{1,0:T(1,128)}) custom-call(f32[4,336,128]{2,1,0:T(8,128)} %pad_maximum_fusion.pieces), custom_call_target="tpu_custom_call" | custom-call | tf_op jit(solution)/shard_map/unpack/pallas_call | solution.py:667
  153.6 1.5 copy.33
  155.2 1.4 copy.32
  156.6 1.2 dynamic-slice_bitcast_fusion
Async XLA Ops:
  15.4 31.8 %all-to-all-start = ((f32[8,16,32,128]{3,2,1,0:T(8,128)}), f32[8,16,32,128]{3,2,1,0:T(8,128)S(1)}, u32[]{:S(2)}, u32[]{:S(2)}) async-start(f32[8,16,32,128]{3,2,1,0:T(8,128)} %bitcast.16), calls=%async_computation | async-start | bytes 4194304 | tf_op jit(solution)/shard_map/all_to_all | solution.py:541
  47.2 1.3 copy-start
  92.7 30.4 %copy-start.1 = (f32[16]{0:T(128)S(1)}, f32[16]{0:T(128)}, u32[]{:S(2)}) copy-start(f32[16]{0:T(128)} %param.23) | copy-start | bytes 196
  100.4 7.3 %collective-permute-start = (f32[336,128]{1,0:T(8,128)}, f32[336,128]{1,0:T(8,128)S(1)}, u32[]{:S(2)}, u32[]{:S(2)}) collective-permute-start(f32[336,128]{1,0:T(8,128)} %filter_gradients.1), channel_id=1, source_target_pairs={{0,4},{4,8},{8,12},{12,16},{16,20},{20,24},{24,28},{28,0},{1,5},{5... | collective-permute-start | bytes 516104 | tf_op jit(solution)/shard_map/ppermute | solution.py:493
  100.4 8.5 %collective-permute-start.1 = (f32[336,128]{1,0:T(8,128)}, f32[336,128]{1,0:T(8,128)S(1)}, u32[]{:S(2)}, u32[]{:S(2)}) collective-permute-start(f32[336,128]{1,0:T(8,128)} %filter_gradients.1), channel_id=1, source_target_pairs={{0,8},{4,12},{8,16},{12,20},{16,24},{20,28},{24,0},{28,4},{1,9},{5... | collective-permute-start | bytes 516104 | tf_op jit(solution)/shard_map/ppermute | solution.py:493
  101.0 14.5 %collective-permute-start.2 = (f32[336,128]{1,0:T(8,128)}, f32[336,128]{1,0:T(8,128)S(1)}, u32[]{:S(2)}, u32[]{:S(2)}) collective-permute-start(f32[336,128]{1,0:T(8,128)} %filter_gradients.1), channel_id=1, source_target_pairs={{0,12},{4,16},{8,20},{12,24},{16,28},{20,0},{24,4},{28,8},{1,13},{... | collective-permute-start | bytes 516104 | tf_op jit(solution)/shard_map/ppermute | solution.py:493
  102.4 13.2 %collective-permute-start.3 = (f32[336,128]{1,0:T(8,128)}, f32[336,128]{1,0:T(8,128)S(1)}, u32[]{:S(2)}, u32[]{:S(2)}) collective-permute-start(f32[336,128]{1,0:T(8,128)} %filter_gradients.1), channel_id=1, source_target_pairs={{0,16},{4,20},{8,24},{12,28},{16,0},{20,4},{24,8},{28,12},{1,17},{... | collective-permute-start | bytes 516104 | tf_op jit(solution)/shard_map/ppermute | solution.py:493
  103.8 13.5 %collective-permute-start.4 = (f32[336,128]{1,0:T(8,128)}, f32[336,128]{1,0:T(8,128)S(1)}, u32[]{:S(2)}, u32[]{:S(2)}) collective-permute-start(f32[336,128]{1,0:T(8,128)} %filter_gradients.1), channel_id=1, source_target_pairs={{0,20},{4,24},{8,28},{12,0},{16,4},{20,8},{24,12},{28,16},{1,21},{... | collective-permute-start | bytes 516104 | tf_op jit(solution)/shard_map/ppermute | solution.py:493
  107.6 9.7 %collective-permute-start.5 = (f32[336,128]{1,0:T(8,128)}, f32[336,128]{1,0:T(8,128)S(1)}, u32[]{:S(2)}, u32[]{:S(2)}) collective-permute-start(f32[336,128]{1,0:T(8,128)} %filter_gradients.1), channel_id=1, source_target_pairs={{0,24},{4,28},{8,0},{12,4},{16,8},{20,12},{24,16},{28,20},{1,25},{... | collective-permute-start | bytes 516104 | tf_op jit(solution)/shard_map/ppermute | solution.py:493
  108.9 8.5 %collective-permute-start.6 = (f32[336,128]{1,0:T(8,128)}, f32[336,128]{1,0:T(8,128)S(1)}, u32[]{:S(2)}, u32[]{:S(2)}) collective-permute-start(f32[336,128]{1,0:T(8,128)} %filter_gradients.1), channel_id=1, source_target_pairs={{0,28},{4,0},{8,4},{12,8},{16,12},{20,16},{24,20},{28,24},{1,29},{... | collective-permute-start | bytes 516104 | tf_op jit(solution)/shard_map/ppermute | solution.py:493
  118.4 32.4 %collective-permute-start.9 = (f32[336,128]{1,0:T(8,128)S(1)}, f32[336,128]{1,0:T(8,128)S(1)}, u32[]{:S(2)}, u32[]{:S(2)}) collective-permute-start(f32[336,128]{1,0:T(8,128)S(1)} %add_add_fusion), channel_id=1, source_target_pairs={{0,3},{1,0},{2,1},{3,2},{4,7},{5,4},{6,5},{7,6},{8,11},{9,8},{10,9... | collective-permute-start | bytes 516104 | tf_op jit(solution)/shard_map/ppermute | solution.py:493
  122.1 28.8 %collective-permute-start.7 = (f32[336,128]{1,0:T(8,128)S(1)}, f32[336,128]{1,0:T(8,128)S(1)}, u32[]{:S(2)}, u32[]{:S(2)}) collective-permute-start(f32[336,128]{1,0:T(8,128)S(1)} %add_add_fusion), channel_id=1, source_target_pairs={{0,1},{1,2},{2,3},{3,0},{4,5},{5,6},{6,7},{7,4},{8,9},{9,10},{10,1... | collective-permute-start | bytes 516104 | tf_op jit(solution)/shard_map/ppermute | solution.py:493
  122.1 28.8 %collective-permute-start.8 = (f32[336,128]{1,0:T(8,128)S(1)}, f32[336,128]{1,0:T(8,128)S(1)}, u32[]{:S(2)}, u32[]{:S(2)}) collective-permute-start(f32[336,128]{1,0:T(8,128)S(1)} %add_add_fusion), channel_id=1, source_target_pairs={{0,2},{1,3},{2,0},{3,1},{4,6},{5,7},{6,4},{7,5},{8,10},{9,11},{10,... | collective-permute-start | bytes 516104 | tf_op jit(solution)/shard_map/ppermute | solution.py:493
